TPU v7x, 512 devices: a whole 4x4x16 slice. The times are simulated.
512 devices in a mesh: rows: 64 (over z, y), cols: 8 (over x, core).
Axes of the slice: x: 4, y: 4, z: 16, core: 2. Of those that a mesh axis runs over, the one named last changes fastest.
Arguments:
- sens_base: bfloat16 [524288, 1024], P('rows', 'cols'), may hold values from -0.14157282 to 0.14157282
- design_field: float32 [512, 1024], P('rows'), may hold values from -3 to 3
- gradient: bfloat16 [512, 1024], P('rows'), may hold values from -6 to 6
- tile_index: int32 [1024], P('cols'), may hold values from 0 to 31
- type_codes: int32 [1024], P('cols'), may hold values from 0 to 2
Outputs:
- r_panels: float32 [512, 1024], P(None, 'cols')
- multipliers: float32 [512], replicated
Inputs may be any that keep to these rules, and one draw needn't show every extreme that they name: `tile_index`: each constraint names one support tile.
All inputs are finite; a program needn't handle non-finite values.
Results may differ from a plain program's by a relative error of at most 0.0003.
The roundings to bfloat16 on the way count: a program that leaves them out, or rounds other values in their place, can miss the bound.
Values may be sent and summed in bfloat16 or wider, within the bound.
A program may use at most 64 MiB of HBM per device.

v0:
```python
import math
import jax
import jax.numpy as jnp
from jax import lax
from jax.sharding import PartitionSpec as P

TILE = 128
PW = 256


def padded_2(cells, sides, width):
    for axis, dim in sides:
        count = lax.axis_size(axis)
        ends = count - 1
        head = lax.slice_in_dim(cells, 0, width, axis=dim)
        tail = lax.slice_in_dim(cells, cells.shape[dim] - width, cells.shape[dim], axis=dim)
        cells = jnp.concatenate(
            [
                lax.ppermute(tail, axis, [(i, (i + 1) % count) for i in range(ends)]),
                cells,
                lax.ppermute(head, axis, [((i + 1) % count, i) for i in range(ends)]),
            ],
            axis=dim,
        )
    return cells


def assemble(base_cols, tile_cols, type_cols, stencils, cell_tile):
    kinds_all = jnp.arange(3, dtype=jnp.int32)
    chooser = (type_cols[None, :] == kinds_all[:, None]).astype(jnp.float32)
    picked = lax.dot_general(
        stencils,
        chooser,
        (((0,), (0,)), ((), ())),
        precision=lax.Precision.HIGHEST,
        preferred_element_type=jnp.float32,
    )
    inside = cell_tile[:, None] == tile_cols[None, :]
    total = base_cols.astype(jnp.float32) + jnp.where(inside, picked / TILE, 0.0)
    return total.astype(jnp.bfloat16)


def matmul(left, right):
    return jnp.dot(left, right, precision=lax.Precision.HIGHEST, preferred_element_type=jnp.float32)


def small_factor(matrix):
    order = matrix.shape[0]
    positions = jnp.arange(order, dtype=jnp.int32)

    def column_step(index_col, carry):
        working, lower = carry
        column = lax.dynamic_slice_in_dim(working, index_col, 1, 1)[:, 0]
        pivot = jnp.sqrt(lax.dynamic_slice_in_dim(column, index_col, 1, 0)[0])
        column = jnp.where(positions >= index_col, column / pivot, 0.0)
        lower = jnp.where(positions[None, :] == index_col, column[:, None], lower)
        working = working - column[:, None] * column[None, :]
        return (working, lower)

    return lax.fori_loop(0, order, column_step, (matrix, jnp.zeros_like(matrix)))[1]


def small_inverse(lower):
    order = lower.shape[0]
    positions = jnp.arange(order, dtype=jnp.int32)
    right = jnp.eye(order, dtype=jnp.float32)

    def row_step(index_row, carry):
        rest, solved = carry
        column = lax.dynamic_slice_in_dim(lower, index_row, 1, 1)[:, 0]
        pivot = lax.dynamic_slice_in_dim(column, index_row, 1, 0)[0]
        value = lax.dynamic_slice_in_dim(rest, index_row, 1, 0) / pivot
        solved = jnp.where(positions[:, None] == index_row, value, solved)
        below = jnp.where(positions > index_row, column, 0.0)
        rest = rest - below[:, None] * value
        return (rest, solved)

    return lax.fori_loop(0, order, row_step, (right, jnp.zeros_like(right)))[1]


def factor_lower(matrix):
    order = matrix.shape[0]
    width = math.gcd(order, 32)
    working = matrix
    lower = jnp.zeros_like(matrix)
    inverses = []
    for block_num in range(order // width):
        start = block_num * width
        diag_lower = small_factor(working[:width, :width])
        diag_inverse = small_inverse(diag_lower)
        inverses.append(diag_inverse)
        lower = lower.at[start : start + width, start : start + width].set(diag_lower)
        if start + width < order:
            panel = matmul(working[width:, :width], diag_inverse.T)
            lower = lower.at[start + width :, start : start + width].set(panel)
            working = working[width:, width:] - matmul(panel, panel.T)
    return (lower, inverses)


def solve_forward(lower, inverses, right):
    width = inverses[0].shape[0]
    solved = []
    for block_num in range(len(inverses)):
        start = block_num * width
        rest = right[start : start + width]
        if block_num > 0:
            rest = rest - matmul(
                lower[start : start + width, :start], jnp.concatenate(solved, axis=0)
            )
        solved.append(matmul(inverses[block_num], rest))
    return jnp.concatenate(solved, axis=0)


def solve_backward(lower, inverses, right):
    width = inverses[0].shape[0]
    order = lower.shape[0]
    solved = []
    for block_num in reversed(range(len(inverses))):
        start = block_num * width
        rest = right[start : start + width]
        if start + width < order:
            rest = rest - matmul(
                lower[start + width :, start : start + width].T, jnp.concatenate(solved, axis=0)
            )
        solved.insert(0, matmul(inverses[block_num].T, rest))
    return jnp.concatenate(solved, axis=0)


def shards(sens_base, design_field, gradient, tile_index, type_codes):
    rows_here = design_field.shape[0]
    grid_width = design_field.shape[1]
    cols_here = sens_base.shape[1]
    factored = 2 * PW
    padded = padded_2(design_field, (("rows", 0),), 1)
    padded = jnp.pad(padded, ((0, 0), (1, 1)))
    north_cells = padded[:-2, 1:-1]
    south_cells = padded[2:, 1:-1]
    west_cells = padded[1:-1, :-2]
    east_cells = padded[1:-1, 2:]
    laplace = 4.0 * design_field - (north_cells + south_cells + west_cells + east_cells)
    slope_x = 0.5 * (east_cells - west_cells)
    slope_y = 0.5 * (south_cells - north_cells)
    stencils = jnp.stack([laplace, slope_x, slope_y]).reshape(3, -1)
    row_glob = lax.axis_index("rows") * rows_here + jnp.arange(rows_here, dtype=jnp.int32)
    col_ids = jnp.arange(grid_width, dtype=jnp.int32) // TILE
    cell_tile = ((row_glob // TILE)[:, None] * (grid_width // TILE) + col_ids[None, :]).reshape(-1)
    local_jac = assemble(sens_base, tile_index, type_codes, stencils, cell_tile)
    grad_flat = gradient.reshape(-1)
    row_major = lax.all_to_all(local_jac, "cols", split_axis=0, concat_axis=1, tiled=True)
    row_piece = row_major.shape[0]
    grad_part = lax.dynamic_slice_in_dim(
        grad_flat, lax.axis_index("cols") * row_piece, row_piece, 0
    )
    leading = row_major[:, :factored]
    gram_block = lax.dot_general(
        leading, row_major, (((0,), (0,)), ((), ())), preferred_element_type=jnp.float32
    )
    projected = jnp.dot(grad_part, leading, preferred_element_type=jnp.float32)
    gram_block, projected = lax.psum((gram_block, projected), ("rows", "cols"))
    gram_head = gram_block[:, :factored]
    gram_own = lax.dynamic_slice_in_dim(
        gram_block, lax.axis_index("cols") * cols_here, cols_here, 1
    )
    lower_chol, inverses = factor_lower(gram_head)
    r_panels = solve_forward(lower_chol, inverses, gram_own)
    half_solved = solve_forward(lower_chol, inverses, projected[:, None])
    multipliers = solve_backward(lower_chol, inverses, half_solved)[:, 0]
    return (r_panels, multipliers)


def solution(mesh):
    placed = (P("rows", "cols"), P("rows", None), P("rows", None), P("cols"), P("cols"))
    return jax.shard_map(
        shards, mesh=mesh, in_specs=placed, out_specs=(P(None, "cols"), P()), check_vma=False
    )
```

profile of v0, /device:TPU:1, one launch (start us, length us, event | category | flops | bytes accessed | tf_op | source)
XLA Modules:
  0.0 2140.8 jit_solution(14819654451309352459)
XLA Ops:
  68.0 110.2 %psum.15 = f32[512]{0:T(512)S(1)} all-reduce(f32[512]{0:T(512)S(1)} %bitcast.1236), channel_id=1, replica_groups=mesh['rows'=64,'cols'=8] {'rows','cols'}, use_global_device_ids=true, to_apply=%region_65.66 | all-reduce | flops 512 | bytes 4096 | tf_op jit(solution)/shard_map/psum | solution.py:159
  178.3 367.6 %all-reduce.4.cloned.1.call-done = f32[512,1024]{1,0:T(8,128)} async-done(((f32[512,1024]{1,0:T(8,128)}), f32[512,1024]{1,0:T(8,128)}) %all-reduce.4.cloned.1.call-update) | async-done | bytes 2097168 | tf_op jit(solution)/shard_map/psum | solution.py:159
  546.7 45.5 %while.671 = (s32[]{:T(128)}, f32[32,32]{0,1:T(8,128)S(1)}, f32[32,32]{0,1:T(8,128)S(1)}, s32[]{:T(128)}, s32[]{:T(128)}, /*index=5*/s32[]{:T(128)}) while((s32[]{:T(128)}, f32[32,32]{0,1:T(8,128)S(1)}, f32[32,32]{0,1:T(8,128)S(1)}, s32[]{:T(128)}, s32[]{:T(128)}, /*index=5*/s32[]{:T(128)}) %tuple.1741), condition=%wide.region_2.3_spmd.clone.clone, body=%wide.region_1.2_spmd.clone.clone.sunk | while | flops 4292 | bytes 19003 | solution.py:60
  639.5 45.0 %while.673 = (s32[]{:T(128)}, f32[32,32]{0,1:T(8,128)S(1)}, f32[32,32]{0,1:T(8,128)S(1)}, s32[]{:T(128)}, s32[]{:T(128)}, /*index=5*/s32[]{:T(128)}) while((s32[]{:T(128)}, f32[32,32]{0,1:T(8,128)S(1)}, f32[32,32]{0,1:T(8,128)S(1)}, s32[]{:T(128)}, s32[]{:T(128)}, /*index=5*/s32[]{:T(128)}) %tuple.1747), condition=%wide.region_6.7_spmd.clone.clone, body=%wide.region_5.6_spmd.clone.clone.sunk | while | flops 4292 | bytes 19003 | solution.py:60
  729.6 45.0 %while.675 = (s32[]{:T(128)}, f32[32,32]{0,1:T(8,128)S(1)}, f32[32,32]{0,1:T(8,128)S(1)}, s32[]{:T(128)}, s32[]{:T(128)}, /*index=5*/s32[]{:T(128)}) while((s32[]{:T(128)}, f32[32,32]{0,1:T(8,128)S(1)}, f32[32,32]{0,1:T(8,128)S(1)}, s32[]{:T(128)}, s32[]{:T(128)}, /*index=5*/s32[]{:T(128)}) %tuple.1753), condition=%wide.region_10.11_spmd.clone.clone, body=%wide.region_9.10_spmd.clone.clone.sunk | while | flops 4292 | bytes 19003 | solution.py:60
  774.6 43.6 %while.676 = (s32[]{:T(128)}, f32[32,32]{1,0:T(8,128)S(1)}, f32[32,32]{1,0:T(8,128)S(1)}, f32[32,32]{0,1:T(8,128)S(1)}, s32[]{:T(128)}, /*index=5*/s32[]{:T(128)}, s32[]{:T(128)}) while((s32[]{:T(128)}, f32[32,32]{1,0:T(8,128)S(1)}, f32[32,32]{1,0:T(8,128)S(1)}, f32[32,32]{0,1:T(8,128)S(1)}, s32[]{:T(128)}, ...), condition=%wide.region_12.13_spmd.clone.clone, body=%wide.region_11.12_spmd.clone.clone.sunk | while | flops 4228 | bytes 18367 | solution.py:78
  819.6 86.6 %while.677 = (s32[]{:T(128)}, f32[32,32]{0,1:T(8,128)S(1)}, f32[32,32]{0,1:T(8,128)}, s32[]{:T(128)}, s32[]{:T(128)}, /*index=5*/s32[]{:T(128)}) while((s32[]{:T(128)}, f32[32,32]{0,1:T(8,128)S(1)}, f32[32,32]{0,1:T(8,128)}, s32[]{:T(128)}, s32[]{:T(128)}, /*index=5*/s32[]{:T(128)}) %tuple.1759), condition=%wide.region_14.15_spmd.clone.clone, body=%wide.region_13.14_spmd.clone.clone.sunk | while | flops 4292 | bytes 19003 | solution.py:60
  917.0 86.4 %while.678 = (s32[]{:T(128)}, f32[32,32]{1,0:T(8,128)S(1)}, f32[32,32]{1,0:T(8,128)S(1)}, f32[32,32]{0,1:T(8,128)}, s32[]{:T(128)}, /*index=5*/s32[]{:T(128)}, s32[]{:T(128)}) while((s32[]{:T(128)}, f32[32,32]{1,0:T(8,128)S(1)}, f32[32,32]{1,0:T(8,128)S(1)}, f32[32,32]{0,1:T(8,128)}, s32[]{:T(128)}, ...), condition=%wide.region_16.17_spmd.clone.clone, body=%wide.region_15.16_spmd.clone.clone.sunk | while | flops 4228 | bytes 18751 | solution.py:78
  1004.5 45.0 %while.679 = (s32[]{:T(128)}, f32[32,32]{0,1:T(8,128)S(1)}, f32[32,32]{0,1:T(8,128)S(1)}, s32[]{:T(128)}, s32[]{:T(128)}, /*index=5*/s32[]{:T(128)}) while((s32[]{:T(128)}, f32[32,32]{0,1:T(8,128)S(1)}, f32[32,32]{0,1:T(8,128)S(1)}, s32[]{:T(128)}, s32[]{:T(128)}, /*index=5*/s32[]{:T(128)}) %tuple.1856), condition=%wide.region_18.19_spmd.clone.clone, body=%wide.region_17.18_spmd.clone.clone.sunk | while | flops 4292 | bytes 19003 | solution.py:60
  1049.5 43.6 %while.680 = (s32[]{:T(128)}, f32[32,32]{1,0:T(8,128)S(1)}, f32[32,32]{1,0:T(8,128)S(1)}, f32[32,32]{0,1:T(8,128)S(1)}, s32[]{:T(128)}, /*index=5*/s32[]{:T(128)}, s32[]{:T(128)}) while((s32[]{:T(128)}, f32[32,32]{1,0:T(8,128)S(1)}, f32[32,32]{1,0:T(8,128)S(1)}, f32[32,32]{0,1:T(8,128)S(1)}, s32[]{:T(128)}, ...), condition=%wide.region_20.21_spmd.clone.clone, body=%wide.region_19.20_spmd.clone.clone.sunk | while | flops 4228 | bytes 18367 | solution.py:78
  1094.1 45.0 %while.681 = (s32[]{:T(128)}, f32[32,32]{0,1:T(8,128)S(1)}, f32[32,32]{0,1:T(8,128)S(1)}, s32[]{:T(128)}, s32[]{:T(128)}, /*index=5*/s32[]{:T(128)}) while((s32[]{:T(128)}, f32[32,32]{0,1:T(8,128)S(1)}, f32[32,32]{0,1:T(8,128)S(1)}, s32[]{:T(128)}, s32[]{:T(128)}, /*index=5*/s32[]{:T(128)}) %tuple.1855), condition=%wide.region_22.23_spmd.clone.clone, body=%wide.region_21.22_spmd.clone.clone.sunk | while | flops 4292 | bytes 19003 | solution.py:60
  1139.2 43.6 %while.682 = (s32[]{:T(128)}, f32[32,32]{1,0:T(8,128)S(1)}, f32[32,32]{1,0:T(8,128)S(1)}, f32[32,32]{0,1:T(8,128)S(1)}, s32[]{:T(128)}, /*index=5*/s32[]{:T(128)}, s32[]{:T(128)}) while((s32[]{:T(128)}, f32[32,32]{1,0:T(8,128)S(1)}, f32[32,32]{1,0:T(8,128)S(1)}, f32[32,32]{0,1:T(8,128)S(1)}, s32[]{:T(128)}, ...), condition=%wide.region_24.25_spmd.clone.clone, body=%wide.region_23.24_spmd.clone.clone.sunk | while | flops 4228 | bytes 18367 | solution.py:78
  1183.8 45.0 %while.683 = (s32[]{:T(128)}, f32[32,32]{0,1:T(8,128)S(1)}, f32[32,32]{0,1:T(8,128)S(1)}, s32[]{:T(128)}, s32[]{:T(128)}, /*index=5*/s32[]{:T(128)}) while((s32[]{:T(128)}, f32[32,32]{0,1:T(8,128)S(1)}, f32[32,32]{0,1:T(8,128)S(1)}, s32[]{:T(128)}, s32[]{:T(128)}, /*index=5*/s32[]{:T(128)}) %tuple.1854), condition=%wide.region_26.27_spmd.clone.clone, body=%wide.region_25.26_spmd.clone.clone.sunk | while | flops 4292 | bytes 19003 | solution.py:60
  1228.8 43.6 %while.684 = (s32[]{:T(128)}, f32[32,32]{1,0:T(8,128)S(1)}, f32[32,32]{1,0:T(8,128)S(1)}, f32[32,32]{0,1:T(8,128)S(1)}, s32[]{:T(128)}, /*index=5*/s32[]{:T(128)}, s32[]{:T(128)}) while((s32[]{:T(128)}, f32[32,32]{1,0:T(8,128)S(1)}, f32[32,32]{1,0:T(8,128)S(1)}, f32[32,32]{0,1:T(8,128)S(1)}, s32[]{:T(128)}, ...), condition=%wide.region_28.29_spmd.clone.clone, body=%wide.region_27.28_spmd.clone.clone.sunk | while | flops 4228 | bytes 18367 | solution.py:78
  1273.3 45.0 %while.685 = (s32[]{:T(128)}, f32[32,32]{0,1:T(8,128)S(1)}, f32[32,32]{0,1:T(8,128)S(1)}, s32[]{:T(128)}, s32[]{:T(128)}, /*index=5*/s32[]{:T(128)}) while((s32[]{:T(128)}, f32[32,32]{0,1:T(8,128)S(1)}, f32[32,32]{0,1:T(8,128)S(1)}, s32[]{:T(128)}, s32[]{:T(128)}, /*index=5*/s32[]{:T(128)}) %tuple.1853), condition=%wide.region_30.31_spmd.clone.clone, body=%wide.region_29.30_spmd.clone.clone.sunk | while | flops 4292 | bytes 19003 | solution.py:60
  1326.6 43.6 %while.686 = (s32[]{:T(128)}, f32[32,32]{1,0:T(8,128)S(1)}, f32[32,32]{1,0:T(8,128)S(1)}, f32[32,32]{0,1:T(8,128)S(1)}, s32[]{:T(128)}, /*index=5*/s32[]{:T(128)}, s32[]{:T(128)}) while((s32[]{:T(128)}, f32[32,32]{1,0:T(8,128)S(1)}, f32[32,32]{1,0:T(8,128)S(1)}, f32[32,32]{0,1:T(8,128)S(1)}, s32[]{:T(128)}, ...), condition=%wide.region_32.33_spmd.clone.clone, body=%wide.region_31.32_spmd.clone.clone.sunk | while | flops 4228 | bytes 18367 | solution.py:78
  1371.0 45.0 %while.687 = (s32[]{:T(128)}, f32[32,32]{0,1:T(8,128)S(1)}, f32[32,32]{0,1:T(8,128)S(1)}, s32[]{:T(128)}, s32[]{:T(128)}, /*index=5*/s32[]{:T(128)}) while((s32[]{:T(128)}, f32[32,32]{0,1:T(8,128)S(1)}, f32[32,32]{0,1:T(8,128)S(1)}, s32[]{:T(128)}, s32[]{:T(128)}, /*index=5*/s32[]{:T(128)}) %tuple.1789), condition=%wide.region_34.35_spmd.clone.clone, body=%wide.region_33.34_spmd.clone.clone.sunk | while | flops 4292 | bytes 19003 | solution.py:60
  1416.1 43.6 %while.688 = (s32[]{:T(128)}, f32[32,32]{1,0:T(8,128)S(1)}, f32[32,32]{1,0:T(8,128)S(1)}, f32[32,32]{0,1:T(8,128)S(1)}, s32[]{:T(128)}, /*index=5*/s32[]{:T(128)}, s32[]{:T(128)}) while((s32[]{:T(128)}, f32[32,32]{1,0:T(8,128)S(1)}, f32[32,32]{1,0:T(8,128)S(1)}, f32[32,32]{0,1:T(8,128)S(1)}, s32[]{:T(128)}, ...), condition=%wide.region_36.37_spmd.clone.clone, body=%wide.region_35.36_spmd.clone.clone.sunk | while | flops 4228 | bytes 18367 | solution.py:78
  1460.5 45.0 %while.689 = (s32[]{:T(128)}, f32[32,32]{0,1:T(8,128)S(1)}, f32[32,32]{0,1:T(8,128)S(1)}, s32[]{:T(128)}, s32[]{:T(128)}, /*index=5*/s32[]{:T(128)}) while((s32[]{:T(128)}, f32[32,32]{0,1:T(8,128)S(1)}, f32[32,32]{0,1:T(8,128)S(1)}, s32[]{:T(128)}, s32[]{:T(128)}, /*index=5*/s32[]{:T(128)}) %tuple.1795), condition=%wide.region_38.39_spmd.clone.clone, body=%wide.region_37.38_spmd.clone.clone.sunk | while | flops 4292 | bytes 19003 | solution.py:60
  1505.5 43.6 %while.690 = (s32[]{:T(128)}, f32[32,32]{1,0:T(8,128)S(1)}, f32[32,32]{1,0:T(8,128)S(1)}, f32[32,32]{0,1:T(8,128)S(1)}, s32[]{:T(128)}, /*index=5*/s32[]{:T(128)}, s32[]{:T(128)}) while((s32[]{:T(128)}, f32[32,32]{1,0:T(8,128)S(1)}, f32[32,32]{1,0:T(8,128)S(1)}, f32[32,32]{0,1:T(8,128)S(1)}, s32[]{:T(128)}, ...), condition=%wide.region_40.41_spmd.clone.clone, body=%wide.region_39.40_spmd.clone.clone.sunk | while | flops 4228 | bytes 18367 | solution.py:78
  1549.8 45.0 %while.691 = (s32[]{:T(128)}, f32[32,32]{0,1:T(8,128)S(1)}, f32[32,32]{0,1:T(8,128)S(1)}, s32[]{:T(128)}, s32[]{:T(128)}, /*index=5*/s32[]{:T(128)}) while((s32[]{:T(128)}, f32[32,32]{0,1:T(8,128)S(1)}, f32[32,32]{0,1:T(8,128)S(1)}, s32[]{:T(128)}, s32[]{:T(128)}, /*index=5*/s32[]{:T(128)}) %tuple.1801), condition=%wide.region_42.43_spmd.clone.clone, body=%wide.region_41.42_spmd.clone.clone.sunk | while | flops 4292 | bytes 19003 | solution.py:60
  1594.9 43.6 %while.692 = (s32[]{:T(128)}, f32[32,32]{1,0:T(8,128)S(1)}, f32[32,32]{1,0:T(8,128)S(1)}, f32[32,32]{0,1:T(8,128)S(1)}, s32[]{:T(128)}, /*index=5*/s32[]{:T(128)}, s32[]{:T(128)}) while((s32[]{:T(128)}, f32[32,32]{1,0:T(8,128)S(1)}, f32[32,32]{1,0:T(8,128)S(1)}, f32[32,32]{0,1:T(8,128)S(1)}, s32[]{:T(128)}, ...), condition=%wide.region_44.45_spmd.clone.clone, body=%wide.region_43.44_spmd.clone.clone.sunk | while | flops 4228 | bytes 18367 | solution.py:78
  1639.2 45.0 %while.693 = (s32[]{:T(128)}, f32[32,32]{0,1:T(8,128)S(1)}, f32[32,32]{0,1:T(8,128)S(1)}, s32[]{:T(128)}, s32[]{:T(128)}, /*index=5*/s32[]{:T(128)}) while((s32[]{:T(128)}, f32[32,32]{0,1:T(8,128)S(1)}, f32[32,32]{0,1:T(8,128)S(1)}, s32[]{:T(128)}, s32[]{:T(128)}, /*index=5*/s32[]{:T(128)}) %tuple.1807), condition=%wide.region_46.47_spmd.clone.clone, body=%wide.region_45.46_spmd.clone.clone.sunk | while | flops 4292 | bytes 19003 | solution.py:60
  1691.8 43.6 %while.694 = (s32[]{:T(128)}, f32[32,32]{1,0:T(8,128)S(1)}, f32[32,32]{1,0:T(8,128)S(1)}, f32[32,32]{0,1:T(8,128)S(1)}, s32[]{:T(128)}, /*index=5*/s32[]{:T(128)}, s32[]{:T(128)}) while((s32[]{:T(128)}, f32[32,32]{1,0:T(8,128)S(1)}, f32[32,32]{1,0:T(8,128)S(1)}, f32[32,32]{0,1:T(8,128)S(1)}, s32[]{:T(128)}, ...), condition=%wide.region_48.49_spmd.clone.clone, body=%wide.region_47.48_spmd.clone.clone.sunk | while | flops 4228 | bytes 18367 | solution.py:78
  1736.0 45.0 %while.695 = (s32[]{:T(128)}, f32[32,32]{0,1:T(8,128)S(1)}, f32[32,32]{0,1:T(8,128)S(1)}, s32[]{:T(128)}, s32[]{:T(128)}, /*index=5*/s32[]{:T(128)}) while((s32[]{:T(128)}, f32[32,32]{0,1:T(8,128)S(1)}, f32[32,32]{0,1:T(8,128)S(1)}, s32[]{:T(128)}, s32[]{:T(128)}, /*index=5*/s32[]{:T(128)}) %tuple.1813), condition=%wide.region_50.51_spmd.clone.clone, body=%wide.region_49.50_spmd.clone.clone.sunk | while | flops 4292 | bytes 19003 | solution.py:60
  1781.0 43.6 %while.696 = (s32[]{:T(128)}, f32[32,32]{1,0:T(8,128)S(1)}, f32[32,32]{1,0:T(8,128)S(1)}, f32[32,32]{0,1:T(8,128)S(1)}, s32[]{:T(128)}, /*index=5*/s32[]{:T(128)}, s32[]{:T(128)}) while((s32[]{:T(128)}, f32[32,32]{1,0:T(8,128)S(1)}, f32[32,32]{1,0:T(8,128)S(1)}, f32[32,32]{0,1:T(8,128)S(1)}, s32[]{:T(128)}, ...), condition=%wide.region_52.53_spmd.clone.clone, body=%wide.region_51.52_spmd.clone.clone.sunk | while | flops 4228 | bytes 18367 | solution.py:78
  1825.1 45.0 %while.697 = (s32[]{:T(128)}, f32[32,32]{0,1:T(8,128)S(1)}, f32[32,32]{0,1:T(8,128)S(1)}, s32[]{:T(128)}, s32[]{:T(128)}, /*index=5*/s32[]{:T(128)}) while((s32[]{:T(128)}, f32[32,32]{0,1:T(8,128)S(1)}, f32[32,32]{0,1:T(8,128)S(1)}, s32[]{:T(128)}, s32[]{:T(128)}, /*index=5*/s32[]{:T(128)}) %tuple.1819), condition=%wide.region_54.55_spmd.clone.clone, body=%wide.region_53.54_spmd.clone.clone.sunk | while | flops 4292 | bytes 19003 | solution.py:60
  1870.2 43.6 %while.698 = (s32[]{:T(128)}, f32[32,32]{1,0:T(8,128)S(1)}, f32[32,32]{1,0:T(8,128)S(1)}, f32[32,32]{0,1:T(8,128)S(1)}, s32[]{:T(128)}, /*index=5*/s32[]{:T(128)}, s32[]{:T(128)}) while((s32[]{:T(128)}, f32[32,32]{1,0:T(8,128)S(1)}, f32[32,32]{1,0:T(8,128)S(1)}, f32[32,32]{0,1:T(8,128)S(1)}, s32[]{:T(128)}, ...), condition=%wide.region_56.57_spmd.clone.clone, body=%wide.region_55.56_spmd.clone.clone.sunk | while | flops 4228 | bytes 18367 | solution.py:78
  1914.3 45.0 %while.699 = (s32[]{:T(128)}, f32[32,32]{0,1:T(8,128)S(1)}, f32[32,32]{0,1:T(8,128)S(1)}, s32[]{:T(128)}, s32[]{:T(128)}, /*index=5*/s32[]{:T(128)}) while((s32[]{:T(128)}, f32[32,32]{0,1:T(8,128)S(1)}, f32[32,32]{0,1:T(8,128)S(1)}, s32[]{:T(128)}, s32[]{:T(128)}, /*index=5*/s32[]{:T(128)}) %tuple.1825), condition=%wide.region_58.59_spmd.clone.clone, body=%wide.region_57.58_spmd.clone.clone.sunk | while | flops 4292 | bytes 19003 | solution.py:60
  1959.4 43.6 %while.700 = (s32[]{:T(128)}, f32[32,32]{1,0:T(8,128)S(1)}, f32[32,32]{1,0:T(8,128)S(1)}, f32[32,32]{0,1:T(8,128)S(1)}, s32[]{:T(128)}, /*index=5*/s32[]{:T(128)}, s32[]{:T(128)}) while((s32[]{:T(128)}, f32[32,32]{1,0:T(8,128)S(1)}, f32[32,32]{1,0:T(8,128)S(1)}, f32[32,32]{0,1:T(8,128)S(1)}, s32[]{:T(128)}, ...), condition=%wide.region_60.61_spmd.clone.clone, body=%wide.region_59.60_spmd.clone.clone.sunk | while | flops 4228 | bytes 18367 | solution.py:78
  2016.5 45.0 %while.701 = (s32[]{:T(128)}, f32[32,32]{0,1:T(8,128)S(1)}, f32[32,32]{0,1:T(8,128)S(1)}, s32[]{:T(128)}, s32[]{:T(128)}, /*index=5*/s32[]{:T(128)}) while((s32[]{:T(128)}, f32[32,32]{0,1:T(8,128)S(1)}, f32[32,32]{0,1:T(8,128)S(1)}, s32[]{:T(128)}, s32[]{:T(128)}, /*index=5*/s32[]{:T(128)}) %tuple.1857), condition=%wide.region_62.63_spmd.clone.clone, body=%wide.region_61.62_spmd.clone.clone.sunk | while | flops 4292 | bytes 19003 | solution.py:60
  2061.5 43.6 %while.702 = (s32[]{:T(128)}, f32[32,32]{1,0:T(8,128)S(1)}, f32[32,32]{1,0:T(8,128)S(1)}, f32[32,32]{0,1:T(8,128)S(1)}, s32[]{:T(128)}, /*index=5*/s32[]{:T(128)}, s32[]{:T(128)}) while((s32[]{:T(128)}, f32[32,32]{1,0:T(8,128)S(1)}, f32[32,32]{1,0:T(8,128)S(1)}, f32[32,32]{0,1:T(8,128)S(1)}, s32[]{:T(128)}, ...), condition=%wide.region_64.65_spmd.clone.clone, body=%wide.region_63.64_spmd.clone.clone.sunk | while | flops 4228 | bytes 18367 | solution.py:78
  (5438 shorter events, 1352.4 us)
Async XLA Ops:
  7.2 538.7 %all-reduce.4.cloned.1.call-start = ((), (), s32[]{:S(2)}) async-start(), calls=%async_computation.1 | async-start | bytes 4194304 | tf_op jit(solution)/shard_map/psum | solution.py:159
  8.1 5.4 collective-permute-start
  12.1 4.4 collective-permute-start.1
  62.1 1.3 copy-start.15
  66.1 0.7 copy-start.24
  66.1 1.6 copy-start.16
  66.1 573.3 %copy-start = (f32[32,32]{1,0:T(8,128)}, f32[32,32]{1,0:T(8,128)S(1)}, u32[]{:S(2)}) copy-start(f32[32,32]{1,0:T(8,128)S(1)} %fusion.258) | copy-start | bytes 12292
  639.5 135.1 %copy-start.2 = (f32[32,32]{1,0:T(8,128)S(1)}, f32[32,32]{1,0:T(8,128)}, u32[]{:S(2)}) copy-start(f32[32,32]{1,0:T(8,128)} %copy-done) | copy-start | bytes 12292
  728.2 91.3 %copy-start.22 = (f32[32,32]{0,1:T(8,128)}, f32[32,32]{0,1:T(8,128)S(1)}, u32[]{:S(2)}) copy-start(f32[32,32]{0,1:T(8,128)S(1)} %get-tuple-element.7857) | copy-start | bytes 12292
  818.2 1.4 copy-start.21
  818.6 98.3 %copy-start.3 = (f32[32,32]{1,0:T(8,128)S(1)}, f32[32,32]{1,0:T(8,128)}, u32[]{:S(2)}) copy-start(f32[32,32]{1,0:T(8,128)} %copy-done) | copy-start | bytes 12292
  819.6 184.9 %copy-start.20 = (f32[32,32]{0,1:T(8,128)S(1)}, f32[32,32]{0,1:T(8,128)}, u32[]{:S(2)}) copy-start(f32[32,32]{0,1:T(8,128)} %custom-call.8) | copy-start | bytes 12292
  906.2 143.3 %copy-start.4 = (f32[32,32]{1,0:T(8,128)S(1)}, f32[32,32]{1,0:T(8,128)}, u32[]{:S(2)}) copy-start(f32[32,32]{1,0:T(8,128)} %copy-done) | copy-start | bytes 12292
  1003.3 90.8 %copy-start.19 = (f32[32,32]{0,1:T(8,128)S(1)}, f32[32,32]{0,1:T(8,128)}, u32[]{:S(2)}) copy-start(f32[32,32]{0,1:T(8,128)} %custom-call.10) | copy-start | bytes 12292
  1003.7 135.5 %copy-start.5 = (f32[32,32]{1,0:T(8,128)S(1)}, f32[32,32]{1,0:T(8,128)}, u32[]{:S(2)}) copy-start(f32[32,32]{1,0:T(8,128)} %copy-done) | copy-start | bytes 12292
  1093.1 90.7 %copy-start.18 = (f32[32,32]{0,1:T(8,128)S(1)}, f32[32,32]{0,1:T(8,128)}, u32[]{:S(2)}) copy-start(f32[32,32]{0,1:T(8,128)} %custom-call.12) | copy-start | bytes 12292
  1093.4 135.4 %copy-start.6 = (f32[32,32]{1,0:T(8,128)S(1)}, f32[32,32]{1,0:T(8,128)}, u32[]{:S(2)}) copy-start(f32[32,32]{1,0:T(8,128)} %copy-done) | copy-start | bytes 12292
  1139.2 134.2 %copy-start.17 = (f32[32,32]{0,1:T(8,128)S(1)}, f32[32,32]{0,1:T(8,128)}, u32[]{:S(2)}) copy-start(f32[32,32]{0,1:T(8,128)} %custom-call.14) | copy-start | bytes 12292
  1183.0 143.6 %copy-start.7 = (f32[32,32]{1,0:T(8,128)S(1)}, f32[32,32]{1,0:T(8,128)}, u32[]{:S(2)}) copy-start(f32[32,32]{1,0:T(8,128)} %copy-done) | copy-start | bytes 12292
  1272.7 143.4 %copy-start.8 = (f32[32,32]{1,0:T(8,128)S(1)}, f32[32,32]{1,0:T(8,128)}, u32[]{:S(2)}) copy-start(f32[32,32]{1,0:T(8,128)} %copy-done) | copy-start | bytes 12292
  1322.9 182.6 %copy-start.9 = (f32[32,32]{1,0:T(8,128)S(1)}, f32[32,32]{1,0:T(8,128)}, u32[]{:S(2)}) copy-start(f32[32,32]{1,0:T(8,128)} %copy-done) | copy-start | bytes 12292
  1371.0 223.8 %copy-start.10 = (f32[32,32]{1,0:T(8,128)S(1)}, f32[32,32]{1,0:T(8,128)}, u32[]{:S(2)}) copy-start(f32[32,32]{1,0:T(8,128)} %copy-done) | copy-start | bytes 12292
  1505.5 186.3 %copy-start.11 = (f32[32,32]{1,0:T(8,128)S(1)}, f32[32,32]{1,0:T(8,128)}, u32[]{:S(2)}) copy-start(f32[32,32]{1,0:T(8,128)} %copy-done) | copy-start | bytes 12292
  1549.8 231.2 %copy-start.12 = (f32[32,32]{1,0:T(8,128)S(1)}, f32[32,32]{1,0:T(8,128)}, u32[]{:S(2)}) copy-start(f32[32,32]{1,0:T(8,128)} %copy-done) | copy-start | bytes 12292
  1638.7 231.5 %copy-start.13 = (f32[32,32]{1,0:T(8,128)S(1)}, f32[32,32]{1,0:T(8,128)}, u32[]{:S(2)}) copy-start(f32[32,32]{1,0:T(8,128)} %copy-done) | copy-start | bytes 12292
  1691.8 267.6 %copy-start.14 = (f32[32,32]{1,0:T(8,128)S(1)}, f32[32,32]{1,0:T(8,128)}, u32[]{:S(2)}) copy-start(f32[32,32]{1,0:T(8,128)} %copy-done) | copy-start | bytes 12292
  1913.8 102.7 %copy-start.23 = (f32[32,32]{0,1:T(8,128)S(1)}, f32[32,32]{0,1:T(8,128)}, u32[]{:S(2)}) copy-start(f32[32,32]{0,1:T(8,128)} %custom-call.30) | copy-start | bytes 12292
  1959.4 102.1 %copy-start.1 = (f32[32,32]{1,0:T(8,128)S(1)}, f32[32,32]{1,0:T(8,128)}, u32[]{:S(2)}) copy-start(f32[32,32]{1,0:T(8,128)} %copy-done) | copy-start | bytes 12292
  2133.2 0.7 copy-start.25
Sparse Core Ops, SparseCore 0:
  66.2 479.6 all-reduce.3
where the time goes:
time: 2160 us; the launch traced here: 2140 us
  local copies, waits for them, and re-layouts  667 us (31%)
  other arithmetic  500 us (23%)
  loops' own time  382 us (18%)
  waiting for transfers between devices  371 us (17%)
  blocking collectives  144 us (7%)
  matrix products  56.1 us (3%)
    another operation x16, loops' own time, small_factor(): lax.fori_loop(0, order, column_step, (matrix, jnp.zeros_like(matrix)))[1]  369 us
    psum x1, waiting for transfers between devices, shards(): gram_block, projected = lax.psum((gram_block, projected), ('rows', 'cols'))  368 us
    mul x1024, other arithmetic, row_step(): rest = rest - below[:, None] * value  363 us
    dynamic_slice x512, local copies, waits for them, and re-layouts, row_step(): pivot = lax.dynamic_slice_in_dim(column, index_row, 1, 0)[0]  322 us
    dynamic_slice x512, local copies, waits for them, and re-layouts, column_step(): pivot = jnp.sqrt(lax.dynamic_slice_in_dim(column, index_col, 1, 0)[0])  301 us
    psum x1, blocking collectives, shards(): gram_block, projected = lax.psum((gram_block, projected), ('rows', 'cols'))  110 us
    select_n x512, other arithmetic, column_step(): lower = jnp.where(positions[None, :] == index_col, column[:, None], lower)  80.9 us
    dot_general x123, matrix products, matmul(): jnp.dot(left, right, precision=lax.Precision.HIGHEST, preferred_element_t...  46.5 us

commit v1 on v0

--- a/solution.py
+++ b/solution.py
@@ -156,7 +156,13 @@
         leading, row_major, (((0,), (0,)), ((), ())), preferred_element_type=jnp.float32
     )
     projected = jnp.dot(grad_part, leading, preferred_element_type=jnp.float32)
-    gram_block, projected = lax.psum((gram_block, projected), ("rows", "cols"))
+
+    def feed_the_pages(here_x, across, lane_axis):
+        for dev_i in (lane_axis, across):
+            here_x = lax.psum(here_x, dev_i)
+        return here_x
+
+    gram_block, projected = feed_the_pages((gram_block, projected), "rows", "cols")
     gram_head = gram_block[:, :factored]
     gram_own = lax.dynamic_slice_in_dim(
         gram_block, lax.axis_index("cols") * cols_here, cols_here, 1

time: 2160 us -> 2040 us (0.944)
  waiting for transfers between devices: 371 us -> 228 us
    psum x1 -> x2, waiting for transfers between devices: 368 us -> 225 us  [feed_the_pages(): here_x = lax.psum(here_x, dev_i)]
    psum x1 -> x2, blocking collectives: 110 us -> 131 us  [feed_the_pages(): here_x = lax.psum(here_x, dev_i)]
where the time goes in v1:
time: 2040 us; the launch traced here: 2020 us
  local copies, waits for them, and re-layouts  667 us (33%)
  other arithmetic  500 us (25%)
  loops' own time  383 us (19%)
  waiting for transfers between devices  228 us (11%)
  blocking collectives  165 us (8%)
  matrix products  56.1 us (3%)
    another operation x16, loops' own time, small_factor(): lax.fori_loop(0, order, column_step, (matrix, jnp.zeros_like(matrix)))[1]  370 us
    mul x1024, other arithmetic, row_step(): rest = rest - below[:, None] * value  363 us
    dynamic_slice x512, local copies, waits for them, and re-layouts, row_step(): pivot = lax.dynamic_slice_in_dim(column, index_row, 1, 0)[0]  322 us
    dynamic_slice x512, local copies, waits for them, and re-layouts, column_step(): pivot = jnp.sqrt(lax.dynamic_slice_in_dim(column, index_col, 1, 0)[0])  302 us
    psum x2, waiting for transfers between devices, feed_the_pages(): here_x = lax.psum(here_x, dev_i)  225 us
    psum x2, blocking collectives, feed_the_pages(): here_x = lax.psum(here_x, dev_i)  131 us
    select_n x512, other arithmetic, column_step(): lower = jnp.where(positions[None, :] == index_col, column[:, None], lower)  80.8 us
    dot_general x123, matrix products, matmul(): jnp.dot(left, right, precision=lax.Precision.HIGHEST, preferred_element_t...  46.5 us

profile of v1, /device:TPU:1, one launch (start us, length us, event | category | flops | bytes accessed | tf_op | source)
XLA Modules:
  0.0 2020.3 jit_solution(425480406392088772)
XLA Ops:
  66.1 82.7 %all-reduce.5.cloned.1.call-done = f32[512,1024]{1,0:T(8,128)} async-done(((f32[512,1024]{1,0:T(8,128)}), f32[512,1024]{1,0:T(8,128)}) %all-reduce.5.cloned.1.call-update) | async-done | bytes 2097168 | tf_op jit(solution)/shard_map/psum | solution.py:162
  163.8 117.0 %psum.31 = f32[512]{0:T(512)S(1)} all-reduce(f32[512]{0:T(512)S(1)} %psum.30), channel_id=1, replica_groups=mesh['rows'=64,'cols'=8] {'rows'}, use_global_device_ids=true, to_apply=%region_67.68 | all-reduce | flops 512 | bytes 4096 | tf_op jit(solution)/shard_map/psum | solution.py:162
  280.8 142.4 %all-reduce.7.cloned.1.call-done = f32[512,1024]{1,0:T(8,128)} async-done(((f32[512,1024]{1,0:T(8,128)}), f32[512,1024]{1,0:T(8,128)}) %all-reduce.7.cloned.1.call-update) | async-done | bytes 2097168 | tf_op jit(solution)/shard_map/psum | solution.py:162
  423.9 47.9 %while.671 = (s32[]{:T(128)}, f32[32,32]{0,1:T(8,128)S(1)}, f32[32,32]{0,1:T(8,128)S(1)}, s32[]{:T(128)}, s32[]{:T(128)}, /*index=5*/s32[]{:T(128)}) while((s32[]{:T(128)}, f32[32,32]{0,1:T(8,128)S(1)}, f32[32,32]{0,1:T(8,128)S(1)}, s32[]{:T(128)}, s32[]{:T(128)}, /*index=5*/s32[]{:T(128)}) %tuple.1741), condition=%wide.region_3.4_spmd.clone.clone, body=%wide.region_2.3_spmd.clone.clone.sunk | while | flops 4292 | bytes 19003 | solution.py:60
  519.2 45.0 %while.673 = (s32[]{:T(128)}, f32[32,32]{0,1:T(8,128)S(1)}, f32[32,32]{0,1:T(8,128)S(1)}, s32[]{:T(128)}, s32[]{:T(128)}, /*index=5*/s32[]{:T(128)}) while((s32[]{:T(128)}, f32[32,32]{0,1:T(8,128)S(1)}, f32[32,32]{0,1:T(8,128)S(1)}, s32[]{:T(128)}, s32[]{:T(128)}, /*index=5*/s32[]{:T(128)}) %tuple.1747), condition=%wide.region_7.8_spmd.clone.clone, body=%wide.region_6.7_spmd.clone.clone.sunk | while | flops 4292 | bytes 19003 | solution.py:60
  609.2 45.0 %while.675 = (s32[]{:T(128)}, f32[32,32]{0,1:T(8,128)S(1)}, f32[32,32]{0,1:T(8,128)S(1)}, s32[]{:T(128)}, s32[]{:T(128)}, /*index=5*/s32[]{:T(128)}) while((s32[]{:T(128)}, f32[32,32]{0,1:T(8,128)S(1)}, f32[32,32]{0,1:T(8,128)S(1)}, s32[]{:T(128)}, s32[]{:T(128)}, /*index=5*/s32[]{:T(128)}) %tuple.1753), condition=%wide.region_11.12_spmd.clone.clone, body=%wide.region_10.11_spmd.clone.clone.sunk | while | flops 4292 | bytes 19003 | solution.py:60
  654.2 43.6 %while.676 = (s32[]{:T(128)}, f32[32,32]{1,0:T(8,128)S(1)}, f32[32,32]{1,0:T(8,128)S(1)}, f32[32,32]{0,1:T(8,128)S(1)}, s32[]{:T(128)}, /*index=5*/s32[]{:T(128)}, s32[]{:T(128)}) while((s32[]{:T(128)}, f32[32,32]{1,0:T(8,128)S(1)}, f32[32,32]{1,0:T(8,128)S(1)}, f32[32,32]{0,1:T(8,128)S(1)}, s32[]{:T(128)}, ...), condition=%wide.region_13.14_spmd.clone.clone, body=%wide.region_12.13_spmd.clone.clone.sunk | while | flops 4228 | bytes 18367 | solution.py:78
  699.2 86.5 %while.677 = (s32[]{:T(128)}, f32[32,32]{0,1:T(8,128)S(1)}, f32[32,32]{0,1:T(8,128)}, s32[]{:T(128)}, s32[]{:T(128)}, /*index=5*/s32[]{:T(128)}) while((s32[]{:T(128)}, f32[32,32]{0,1:T(8,128)S(1)}, f32[32,32]{0,1:T(8,128)}, s32[]{:T(128)}, s32[]{:T(128)}, /*index=5*/s32[]{:T(128)}) %tuple.1759), condition=%wide.region_15.16_spmd.clone.clone, body=%wide.region_14.15_spmd.clone.clone.sunk | while | flops 4292 | bytes 19003 | solution.py:60
  796.5 86.4 %while.678 = (s32[]{:T(128)}, f32[32,32]{1,0:T(8,128)S(1)}, f32[32,32]{1,0:T(8,128)S(1)}, f32[32,32]{0,1:T(8,128)}, s32[]{:T(128)}, /*index=5*/s32[]{:T(128)}, s32[]{:T(128)}) while((s32[]{:T(128)}, f32[32,32]{1,0:T(8,128)S(1)}, f32[32,32]{1,0:T(8,128)S(1)}, f32[32,32]{0,1:T(8,128)}, s32[]{:T(128)}, ...), condition=%wide.region_17.18_spmd.clone.clone, body=%wide.region_16.17_spmd.clone.clone.sunk | while | flops 4228 | bytes 18751 | solution.py:78
  884.0 45.0 %while.679 = (s32[]{:T(128)}, f32[32,32]{0,1:T(8,128)S(1)}, f32[32,32]{0,1:T(8,128)S(1)}, s32[]{:T(128)}, s32[]{:T(128)}, /*index=5*/s32[]{:T(128)}) while((s32[]{:T(128)}, f32[32,32]{0,1:T(8,128)S(1)}, f32[32,32]{0,1:T(8,128)S(1)}, s32[]{:T(128)}, s32[]{:T(128)}, /*index=5*/s32[]{:T(128)}) %tuple.1858), condition=%wide.region_19.20_spmd.clone.clone, body=%wide.region_18.19_spmd.clone.clone.sunk | while | flops 4292 | bytes 19003 | solution.py:60
  929.0 43.6 %while.680 = (s32[]{:T(128)}, f32[32,32]{1,0:T(8,128)S(1)}, f32[32,32]{1,0:T(8,128)S(1)}, f32[32,32]{0,1:T(8,128)S(1)}, s32[]{:T(128)}, /*index=5*/s32[]{:T(128)}, s32[]{:T(128)}) while((s32[]{:T(128)}, f32[32,32]{1,0:T(8,128)S(1)}, f32[32,32]{1,0:T(8,128)S(1)}, f32[32,32]{0,1:T(8,128)S(1)}, s32[]{:T(128)}, ...), condition=%wide.region_21.22_spmd.clone.clone, body=%wide.region_20.21_spmd.clone.clone.sunk | while | flops 4228 | bytes 18367 | solution.py:78
  973.7 45.0 %while.681 = (s32[]{:T(128)}, f32[32,32]{0,1:T(8,128)S(1)}, f32[32,32]{0,1:T(8,128)S(1)}, s32[]{:T(128)}, s32[]{:T(128)}, /*index=5*/s32[]{:T(128)}) while((s32[]{:T(128)}, f32[32,32]{0,1:T(8,128)S(1)}, f32[32,32]{0,1:T(8,128)S(1)}, s32[]{:T(128)}, s32[]{:T(128)}, /*index=5*/s32[]{:T(128)}) %tuple.1857), condition=%wide.region_23.24_spmd.clone.clone, body=%wide.region_22.23_spmd.clone.clone.sunk | while | flops 4292 | bytes 19003 | solution.py:60
  1018.7 43.6 %while.682 = (s32[]{:T(128)}, f32[32,32]{1,0:T(8,128)S(1)}, f32[32,32]{1,0:T(8,128)S(1)}, f32[32,32]{0,1:T(8,128)S(1)}, s32[]{:T(128)}, /*index=5*/s32[]{:T(128)}, s32[]{:T(128)}) while((s32[]{:T(128)}, f32[32,32]{1,0:T(8,128)S(1)}, f32[32,32]{1,0:T(8,128)S(1)}, f32[32,32]{0,1:T(8,128)S(1)}, s32[]{:T(128)}, ...), condition=%wide.region_25.26_spmd.clone.clone, body=%wide.region_24.25_spmd.clone.clone.sunk | while | flops 4228 | bytes 18367 | solution.py:78
  1063.3 45.0 %while.683 = (s32[]{:T(128)}, f32[32,32]{0,1:T(8,128)S(1)}, f32[32,32]{0,1:T(8,128)S(1)}, s32[]{:T(128)}, s32[]{:T(128)}, /*index=5*/s32[]{:T(128)}) while((s32[]{:T(128)}, f32[32,32]{0,1:T(8,128)S(1)}, f32[32,32]{0,1:T(8,128)S(1)}, s32[]{:T(128)}, s32[]{:T(128)}, /*index=5*/s32[]{:T(128)}) %tuple.1856), condition=%wide.region_27.28_spmd.clone.clone, body=%wide.region_26.27_spmd.clone.clone.sunk | while | flops 4292 | bytes 19003 | solution.py:60
  1108.3 43.6 %while.684 = (s32[]{:T(128)}, f32[32,32]{1,0:T(8,128)S(1)}, f32[32,32]{1,0:T(8,128)S(1)}, f32[32,32]{0,1:T(8,128)S(1)}, s32[]{:T(128)}, /*index=5*/s32[]{:T(128)}, s32[]{:T(128)}) while((s32[]{:T(128)}, f32[32,32]{1,0:T(8,128)S(1)}, f32[32,32]{1,0:T(8,128)S(1)}, f32[32,32]{0,1:T(8,128)S(1)}, s32[]{:T(128)}, ...), condition=%wide.region_29.30_spmd.clone.clone, body=%wide.region_28.29_spmd.clone.clone.sunk | while | flops 4228 | bytes 18367 | solution.py:78
  1152.9 45.0 %while.685 = (s32[]{:T(128)}, f32[32,32]{0,1:T(8,128)S(1)}, f32[32,32]{0,1:T(8,128)S(1)}, s32[]{:T(128)}, s32[]{:T(128)}, /*index=5*/s32[]{:T(128)}) while((s32[]{:T(128)}, f32[32,32]{0,1:T(8,128)S(1)}, f32[32,32]{0,1:T(8,128)S(1)}, s32[]{:T(128)}, s32[]{:T(128)}, /*index=5*/s32[]{:T(128)}) %tuple.1855), condition=%wide.region_31.32_spmd.clone.clone, body=%wide.region_30.31_spmd.clone.clone.sunk | while | flops 4292 | bytes 19003 | solution.py:60
  1206.1 43.6 %while.686 = (s32[]{:T(128)}, f32[32,32]{1,0:T(8,128)S(1)}, f32[32,32]{1,0:T(8,128)S(1)}, f32[32,32]{0,1:T(8,128)S(1)}, s32[]{:T(128)}, /*index=5*/s32[]{:T(128)}, s32[]{:T(128)}) while((s32[]{:T(128)}, f32[32,32]{1,0:T(8,128)S(1)}, f32[32,32]{1,0:T(8,128)S(1)}, f32[32,32]{0,1:T(8,128)S(1)}, s32[]{:T(128)}, ...), condition=%wide.region_33.34_spmd.clone.clone, body=%wide.region_32.33_spmd.clone.clone.sunk | while | flops 4228 | bytes 18367 | solution.py:78
  1250.5 45.0 %while.687 = (s32[]{:T(128)}, f32[32,32]{0,1:T(8,128)S(1)}, f32[32,32]{0,1:T(8,128)S(1)}, s32[]{:T(128)}, s32[]{:T(128)}, /*index=5*/s32[]{:T(128)}) while((s32[]{:T(128)}, f32[32,32]{0,1:T(8,128)S(1)}, f32[32,32]{0,1:T(8,128)S(1)}, s32[]{:T(128)}, s32[]{:T(128)}, /*index=5*/s32[]{:T(128)}) %tuple.1789), condition=%wide.region_35.36_spmd.clone.clone, body=%wide.region_34.35_spmd.clone.clone.sunk | while | flops 4292 | bytes 19003 | solution.py:60
  1295.6 43.6 %while.688 = (s32[]{:T(128)}, f32[32,32]{1,0:T(8,128)S(1)}, f32[32,32]{1,0:T(8,128)S(1)}, f32[32,32]{0,1:T(8,128)S(1)}, s32[]{:T(128)}, /*index=5*/s32[]{:T(128)}, s32[]{:T(128)}) while((s32[]{:T(128)}, f32[32,32]{1,0:T(8,128)S(1)}, f32[32,32]{1,0:T(8,128)S(1)}, f32[32,32]{0,1:T(8,128)S(1)}, s32[]{:T(128)}, ...), condition=%wide.region_37.38_spmd.clone.clone, body=%wide.region_36.37_spmd.clone.clone.sunk | while | flops 4228 | bytes 18367 | solution.py:78
  1340.0 45.0 %while.689 = (s32[]{:T(128)}, f32[32,32]{0,1:T(8,128)S(1)}, f32[32,32]{0,1:T(8,128)S(1)}, s32[]{:T(128)}, s32[]{:T(128)}, /*index=5*/s32[]{:T(128)}) while((s32[]{:T(128)}, f32[32,32]{0,1:T(8,128)S(1)}, f32[32,32]{0,1:T(8,128)S(1)}, s32[]{:T(128)}, s32[]{:T(128)}, /*index=5*/s32[]{:T(128)}) %tuple.1795), condition=%wide.region_39.40_spmd.clone.clone, body=%wide.region_38.39_spmd.clone.clone.sunk | while | flops 4292 | bytes 19003 | solution.py:60
  1385.0 43.6 %while.690 = (s32[]{:T(128)}, f32[32,32]{1,0:T(8,128)S(1)}, f32[32,32]{1,0:T(8,128)S(1)}, f32[32,32]{0,1:T(8,128)S(1)}, s32[]{:T(128)}, /*index=5*/s32[]{:T(128)}, s32[]{:T(128)}) while((s32[]{:T(128)}, f32[32,32]{1,0:T(8,128)S(1)}, f32[32,32]{1,0:T(8,128)S(1)}, f32[32,32]{0,1:T(8,128)S(1)}, s32[]{:T(128)}, ...), condition=%wide.region_41.42_spmd.clone.clone, body=%wide.region_40.41_spmd.clone.clone.sunk | while | flops 4228 | bytes 18367 | solution.py:78
  1429.3 45.0 %while.691 = (s32[]{:T(128)}, f32[32,32]{0,1:T(8,128)S(1)}, f32[32,32]{0,1:T(8,128)S(1)}, s32[]{:T(128)}, s32[]{:T(128)}, /*index=5*/s32[]{:T(128)}) while((s32[]{:T(128)}, f32[32,32]{0,1:T(8,128)S(1)}, f32[32,32]{0,1:T(8,128)S(1)}, s32[]{:T(128)}, s32[]{:T(128)}, /*index=5*/s32[]{:T(128)}) %tuple.1801), condition=%wide.region_43.44_spmd.clone.clone, body=%wide.region_42.43_spmd.clone.clone.sunk | while | flops 4292 | bytes 19003 | solution.py:60
  1474.4 43.6 %while.692 = (s32[]{:T(128)}, f32[32,32]{1,0:T(8,128)S(1)}, f32[32,32]{1,0:T(8,128)S(1)}, f32[32,32]{0,1:T(8,128)S(1)}, s32[]{:T(128)}, /*index=5*/s32[]{:T(128)}, s32[]{:T(128)}) while((s32[]{:T(128)}, f32[32,32]{1,0:T(8,128)S(1)}, f32[32,32]{1,0:T(8,128)S(1)}, f32[32,32]{0,1:T(8,128)S(1)}, s32[]{:T(128)}, ...), condition=%wide.region_45.46_spmd.clone.clone, body=%wide.region_44.45_spmd.clone.clone.sunk | while | flops 4228 | bytes 18367 | solution.py:78
  1518.7 45.0 %while.693 = (s32[]{:T(128)}, f32[32,32]{0,1:T(8,128)S(1)}, f32[32,32]{0,1:T(8,128)S(1)}, s32[]{:T(128)}, s32[]{:T(128)}, /*index=5*/s32[]{:T(128)}) while((s32[]{:T(128)}, f32[32,32]{0,1:T(8,128)S(1)}, f32[32,32]{0,1:T(8,128)S(1)}, s32[]{:T(128)}, s32[]{:T(128)}, /*index=5*/s32[]{:T(128)}) %tuple.1807), condition=%wide.region_47.48_spmd.clone.clone, body=%wide.region_46.47_spmd.clone.clone.sunk | while | flops 4292 | bytes 19003 | solution.py:60
  1571.3 43.6 %while.694 = (s32[]{:T(128)}, f32[32,32]{1,0:T(8,128)S(1)}, f32[32,32]{1,0:T(8,128)S(1)}, f32[32,32]{0,1:T(8,128)S(1)}, s32[]{:T(128)}, /*index=5*/s32[]{:T(128)}, s32[]{:T(128)}) while((s32[]{:T(128)}, f32[32,32]{1,0:T(8,128)S(1)}, f32[32,32]{1,0:T(8,128)S(1)}, f32[32,32]{0,1:T(8,128)S(1)}, s32[]{:T(128)}, ...), condition=%wide.region_49.50_spmd.clone.clone, body=%wide.region_48.49_spmd.clone.clone.sunk | while | flops 4228 | bytes 18367 | solution.py:78
  1615.5 45.0 %while.695 = (s32[]{:T(128)}, f32[32,32]{0,1:T(8,128)S(1)}, f32[32,32]{0,1:T(8,128)S(1)}, s32[]{:T(128)}, s32[]{:T(128)}, /*index=5*/s32[]{:T(128)}) while((s32[]{:T(128)}, f32[32,32]{0,1:T(8,128)S(1)}, f32[32,32]{0,1:T(8,128)S(1)}, s32[]{:T(128)}, s32[]{:T(128)}, /*index=5*/s32[]{:T(128)}) %tuple.1813), condition=%wide.region_51.52_spmd.clone.clone, body=%wide.region_50.51_spmd.clone.clone.sunk | while | flops 4292 | bytes 19003 | solution.py:60
  1704.7 45.0 %while.697 = (s32[]{:T(128)}, f32[32,32]{0,1:T(8,128)S(1)}, f32[32,32]{0,1:T(8,128)S(1)}, s32[]{:T(128)}, s32[]{:T(128)}, /*index=5*/s32[]{:T(128)}) while((s32[]{:T(128)}, f32[32,32]{0,1:T(8,128)S(1)}, f32[32,32]{0,1:T(8,128)S(1)}, s32[]{:T(128)}, s32[]{:T(128)}, /*index=5*/s32[]{:T(128)}) %tuple.1819), condition=%wide.region_55.56_spmd.clone.clone, body=%wide.region_54.55_spmd.clone.clone.sunk | while | flops 4292 | bytes 19003 | solution.py:60
  1749.7 43.6 %while.698 = (s32[]{:T(128)}, f32[32,32]{1,0:T(8,128)S(1)}, f32[32,32]{1,0:T(8,128)S(1)}, f32[32,32]{0,1:T(8,128)S(1)}, s32[]{:T(128)}, /*index=5*/s32[]{:T(128)}, s32[]{:T(128)}) while((s32[]{:T(128)}, f32[32,32]{1,0:T(8,128)S(1)}, f32[32,32]{1,0:T(8,128)S(1)}, f32[32,32]{0,1:T(8,128)S(1)}, s32[]{:T(128)}, ...), condition=%wide.region_57.58_spmd.clone.clone, body=%wide.region_56.57_spmd.clone.clone.sunk | while | flops 4228 | bytes 18367 | solution.py:78
  1793.8 45.0 %while.699 = (s32[]{:T(128)}, f32[32,32]{0,1:T(8,128)S(1)}, f32[32,32]{0,1:T(8,128)S(1)}, s32[]{:T(128)}, s32[]{:T(128)}, /*index=5*/s32[]{:T(128)}) while((s32[]{:T(128)}, f32[32,32]{0,1:T(8,128)S(1)}, f32[32,32]{0,1:T(8,128)S(1)}, s32[]{:T(128)}, s32[]{:T(128)}, /*index=5*/s32[]{:T(128)}) %tuple.1825), condition=%wide.region_59.60_spmd.clone.clone, body=%wide.region_58.59_spmd.clone.clone.sunk | while | flops 4292 | bytes 19003 | solution.py:60
  1838.9 43.6 %while.700 = (s32[]{:T(128)}, f32[32,32]{1,0:T(8,128)S(1)}, f32[32,32]{1,0:T(8,128)S(1)}, f32[32,32]{0,1:T(8,128)S(1)}, s32[]{:T(128)}, /*index=5*/s32[]{:T(128)}, s32[]{:T(128)}) while((s32[]{:T(128)}, f32[32,32]{1,0:T(8,128)S(1)}, f32[32,32]{1,0:T(8,128)S(1)}, f32[32,32]{0,1:T(8,128)S(1)}, s32[]{:T(128)}, ...), condition=%wide.region_61.62_spmd.clone.clone, body=%wide.region_60.61_spmd.clone.clone.sunk | while | flops 4228 | bytes 18367 | solution.py:78
  1896.0 45.0 %while.701 = (s32[]{:T(128)}, f32[32,32]{0,1:T(8,128)S(1)}, f32[32,32]{0,1:T(8,128)S(1)}, s32[]{:T(128)}, s32[]{:T(128)}, /*index=5*/s32[]{:T(128)}) while((s32[]{:T(128)}, f32[32,32]{0,1:T(8,128)S(1)}, f32[32,32]{0,1:T(8,128)S(1)}, s32[]{:T(128)}, s32[]{:T(128)}, /*index=5*/s32[]{:T(128)}) %tuple.1859), condition=%wide.region_63.64_spmd.clone.clone, body=%wide.region_62.63_spmd.clone.clone.sunk | while | flops 4292 | bytes 19003 | solution.py:60
  1941.0 43.6 %while.702 = (s32[]{:T(128)}, f32[32,32]{1,0:T(8,128)S(1)}, f32[32,32]{1,0:T(8,128)S(1)}, f32[32,32]{0,1:T(8,128)S(1)}, s32[]{:T(128)}, /*index=5*/s32[]{:T(128)}, s32[]{:T(128)}) while((s32[]{:T(128)}, f32[32,32]{1,0:T(8,128)S(1)}, f32[32,32]{1,0:T(8,128)S(1)}, f32[32,32]{0,1:T(8,128)S(1)}, s32[]{:T(128)}, ...), condition=%wide.region_65.66_spmd.clone.clone, body=%wide.region_64.65_spmd.clone.clone.sunk | while | flops 4228 | bytes 18367 | solution.py:78
  (5442 shorter events, 1410.0 us)
Async XLA Ops:
  7.2 141.7 %all-reduce.5.cloned.1.call-start = ((), (), s32[]{:S(2)}) async-start(), calls=%async_computation.1 | async-start | bytes 4194304 | tf_op jit(solution)/shard_map/psum | solution.py:162
  8.1 5.4 collective-permute-start
  12.1 4.4 collective-permute-start.1
  62.1 1.3 copy-start.15
  66.0 83.2 %copy-start.24 = (bf16[8,1024]{1,0:T(8,128)(2,1)S(1)}, bf16[8,1024]{1,0:T(8,128)(2,1)}, u32[]{:S(2)}) copy-start(bf16[8,1024]{1,0:T(8,128)(2,1)} %param.133) | copy-start | bytes 49156
  66.0 83.2 %copy-start.16 = (bf16[8,1024,128]{1,2,0:T(8,128)(2,1)S(1)}, bf16[8,1024,128]{1,2,0:T(8,128)(2,1)}, u32[]{:S(2)}) copy-start(bf16[8,1024,128]{1,2,0:T(8,128)(2,1)} %copy-done.15) | copy-start | bytes 6291460
  66.1 357.1 %all-reduce.7.cloned.1.call-start = ((), (), s32[]{:S(2)}) async-start(), calls=%async_computation.2 | async-start | bytes 4194304 | tf_op jit(solution)/shard_map/psum | solution.py:162
  148.9 370.2 %copy-start = (f32[32,32]{1,0:T(8,128)}, f32[32,32]{1,0:T(8,128)S(1)}, u32[]{:S(2)}) copy-start(f32[32,32]{1,0:T(8,128)S(1)} %fusion.258) | copy-start | bytes 12292
  519.1 135.1 %copy-start.2 = (f32[32,32]{1,0:T(8,128)S(1)}, f32[32,32]{1,0:T(8,128)}, u32[]{:S(2)}) copy-start(f32[32,32]{1,0:T(8,128)} %copy-done) | copy-start | bytes 12292
  607.8 91.3 %copy-start.22 = (f32[32,32]{0,1:T(8,128)}, f32[32,32]{0,1:T(8,128)S(1)}, u32[]{:S(2)}) copy-start(f32[32,32]{0,1:T(8,128)S(1)} %get-tuple-element.7861) | copy-start | bytes 12292
  697.8 1.4 copy-start.21
  698.2 98.2 %copy-start.3 = (f32[32,32]{1,0:T(8,128)S(1)}, f32[32,32]{1,0:T(8,128)}, u32[]{:S(2)}) copy-start(f32[32,32]{1,0:T(8,128)} %copy-done) | copy-start | bytes 12292
  699.2 184.8 %copy-start.20 = (f32[32,32]{0,1:T(8,128)S(1)}, f32[32,32]{0,1:T(8,128)}, u32[]{:S(2)}) copy-start(f32[32,32]{0,1:T(8,128)} %custom-call.8) | copy-start | bytes 12292
  785.7 143.2 %copy-start.4 = (f32[32,32]{1,0:T(8,128)S(1)}, f32[32,32]{1,0:T(8,128)}, u32[]{:S(2)}) copy-start(f32[32,32]{1,0:T(8,128)} %copy-done) | copy-start | bytes 12292
  882.9 90.8 %copy-start.19 = (f32[32,32]{0,1:T(8,128)S(1)}, f32[32,32]{0,1:T(8,128)}, u32[]{:S(2)}) copy-start(f32[32,32]{0,1:T(8,128)} %custom-call.10) | copy-start | bytes 12292
  883.2 135.5 %copy-start.5 = (f32[32,32]{1,0:T(8,128)S(1)}, f32[32,32]{1,0:T(8,128)}, u32[]{:S(2)}) copy-start(f32[32,32]{1,0:T(8,128)} %copy-done) | copy-start | bytes 12292
  972.6 90.7 %copy-start.18 = (f32[32,32]{0,1:T(8,128)S(1)}, f32[32,32]{0,1:T(8,128)}, u32[]{:S(2)}) copy-start(f32[32,32]{0,1:T(8,128)} %custom-call.12) | copy-start | bytes 12292
  972.9 135.4 %copy-start.6 = (f32[32,32]{1,0:T(8,128)S(1)}, f32[32,32]{1,0:T(8,128)}, u32[]{:S(2)}) copy-start(f32[32,32]{1,0:T(8,128)} %copy-done) | copy-start | bytes 12292
  1018.7 134.2 %copy-start.17 = (f32[32,32]{0,1:T(8,128)S(1)}, f32[32,32]{0,1:T(8,128)}, u32[]{:S(2)}) copy-start(f32[32,32]{0,1:T(8,128)} %custom-call.14) | copy-start | bytes 12292
  1062.6 143.6 %copy-start.7 = (f32[32,32]{1,0:T(8,128)S(1)}, f32[32,32]{1,0:T(8,128)}, u32[]{:S(2)}) copy-start(f32[32,32]{1,0:T(8,128)} %copy-done) | copy-start | bytes 12292
  1152.2 143.4 %copy-start.8 = (f32[32,32]{1,0:T(8,128)S(1)}, f32[32,32]{1,0:T(8,128)}, u32[]{:S(2)}) copy-start(f32[32,32]{1,0:T(8,128)} %copy-done) | copy-start | bytes 12292
  1202.4 182.6 %copy-start.9 = (f32[32,32]{1,0:T(8,128)S(1)}, f32[32,32]{1,0:T(8,128)}, u32[]{:S(2)}) copy-start(f32[32,32]{1,0:T(8,128)} %copy-done) | copy-start | bytes 12292
  1250.5 223.8 %copy-start.10 = (f32[32,32]{1,0:T(8,128)S(1)}, f32[32,32]{1,0:T(8,128)}, u32[]{:S(2)}) copy-start(f32[32,32]{1,0:T(8,128)} %copy-done) | copy-start | bytes 12292
  1385.0 186.3 %copy-start.11 = (f32[32,32]{1,0:T(8,128)S(1)}, f32[32,32]{1,0:T(8,128)}, u32[]{:S(2)}) copy-start(f32[32,32]{1,0:T(8,128)} %copy-done) | copy-start | bytes 12292
  1429.3 231.2 %copy-start.12 = (f32[32,32]{1,0:T(8,128)S(1)}, f32[32,32]{1,0:T(8,128)}, u32[]{:S(2)}) copy-start(f32[32,32]{1,0:T(8,128)} %copy-done) | copy-start | bytes 12292
  1518.2 231.5 %copy-start.13 = (f32[32,32]{1,0:T(8,128)S(1)}, f32[32,32]{1,0:T(8,128)}, u32[]{:S(2)}) copy-start(f32[32,32]{1,0:T(8,128)} %copy-done) | copy-start | bytes 12292
  1571.3 267.6 %copy-start.14 = (f32[32,32]{1,0:T(8,128)S(1)}, f32[32,32]{1,0:T(8,128)}, u32[]{:S(2)}) copy-start(f32[32,32]{1,0:T(8,128)} %copy-done) | copy-start | bytes 12292
  1793.3 102.7 %copy-start.23 = (f32[32,32]{0,1:T(8,128)S(1)}, f32[32,32]{0,1:T(8,128)}, u32[]{:S(2)}) copy-start(f32[32,32]{0,1:T(8,128)} %custom-call.30) | copy-start | bytes 12292
  1838.9 102.1 %copy-start.1 = (f32[32,32]{1,0:T(8,128)S(1)}, f32[32,32]{1,0:T(8,128)}, u32[]{:S(2)}) copy-start(f32[32,32]{1,0:T(8,128)} %copy-done) | copy-start | bytes 12292
  2012.7 0.7 copy-start.25
Sparse Core Ops, SparseCore 0:
  66.2 82.5 all-reduce.4
  152.2 270.8 all-reduce.6
